TPU v7x, 32 devices: a whole 2x2x4 slice. The times are simulated.
32 devices in a mesh: grp: 2 (over core), ctx: 4 (over z), wsh: 4 (over y, x).
Axes of the slice: x: 2, y: 2, z: 4, core: 2. Of those that a mesh axis runs over, the one named last changes fastest.
Arguments:
- tokens: bfloat16 [6144, 1152], P(('grp', 'ctx', 'wsh')), may hold values from -6 to 6
- segment_ids: int32 [6144], P(('grp', 'ctx', 'wsh')), may hold values from 0 to 1, as said below
- positions: int32 [6144], P(('grp', 'ctx', 'wsh')), may hold values from 0 to 3071, as said below
- attend_gain: float32 [1152], replicated, may hold values from 0.5 to 1.5
- query_key_value: bfloat16 [1152, 1920], P('wsh'), may hold values from -0.25 to 0.25
- attend_out: bfloat16 [1152, 1152], P('wsh'), may hold values from -2 to 2
- feed_gain: float32 [1152], replicated, may hold values from 0.5 to 1.5
- gate_up: bfloat16 [1152, 6144], P('wsh'), may hold values from -0.1875 to 0.1875
- down_weight: bfloat16 [3072, 1152], P('wsh'), may hold values from -0.4375 to 0.4375
- upstream: bfloat16 [6144, 1152], P(('grp', 'ctx', 'wsh')), may hold values from -6 to 6
Outputs:
- activations: bfloat16 [6144, 1152], P(('grp', 'ctx', 'wsh'))
- input_grad: float32 [6144, 1152], P(('grp', 'ctx', 'wsh'))
- query_key_value_grad: float32 [1152, 1920], P(('ctx', 'wsh'))
- attend_out_grad: float32 [1152, 1152], P(('ctx', 'wsh'))
- gate_up_grad: float32 [1152, 6144], P(('ctx', 'wsh'))
- down_weight_grad: float32 [3072, 1152], P(('ctx', 'wsh'))
- attend_gain_grad: float32 [1152], P(('ctx', 'wsh'))
- feed_gain_grad: float32 [1152], P(('ctx', 'wsh'))
Inputs may be any that keep to these rules, and one draw needn't show every extreme that they name: `segment_ids`: in each group of 3072 rows the aligned runs of 96 rows are the runs of 96 consecutive tokens of that group's token stream, in some order, each once; the stream is the prompt of 2048 tokens (segment 0) followed by 1 continuations of 1024 tokens (segments 1 to 1). `positions`: matching segment_ids: a prompt token's position is its index in the prompt; a continuation token's position is 2048 plus its index in its continuation.
All inputs are finite; a program needn't handle non-finite values.
Results may differ from a plain program's by a relative error of at most 0.02.
Values may be sent and summed in bfloat16 or wider, within the bound.
A program may use at most 256 MiB of HBM per device.

v0:
```python
import math
import jax
import jax.numpy as jnp
from jax import lax
from jax.sharding import PartitionSpec as P

HEADS = 18
KV_HEADS = 6
HEAD_DIM = 64
FF = 3072
KTILE = 1024
QW = 1152
KW = 384
EPSILON = 1e-05


def rope_angles(positions):
    halfway = HEAD_DIM // 2
    frequency = jnp.exp(jnp.arange(halfway, dtype=jnp.float32) * (-math.log(10000.0) / halfway))
    angles = positions.astype(jnp.float32)[:, None] * frequency[None, :]
    return (jnp.cos(angles), jnp.sin(angles))


def rotate(tensor, cosine, sine_table):
    halfway = tensor.shape[-1] // 2
    first_half = tensor[..., :halfway]
    second_half = tensor[..., halfway:]
    cos_wide = cosine[:, None, :]
    sin_wide = sine_table[:, None, :]
    return jnp.concatenate(
        [
            first_half * cos_wide - second_half * sin_wide,
            second_half * cos_wide + first_half * sin_wide,
        ],
        axis=-1,
    )


def unrotate(gradient, cosine, sine_table):
    halfway = gradient.shape[-1] // 2
    first_half = gradient[..., :halfway]
    second_half = gradient[..., halfway:]
    cos_wide = cosine[:, None, :]
    sin_wide = sine_table[:, None, :]
    return jnp.concatenate(
        [
            first_half * cos_wide + second_half * sin_wide,
            second_half * cos_wide - first_half * sin_wide,
        ],
        axis=-1,
    )


def rms_factor(values):
    return lax.rsqrt(jnp.mean(values * values, axis=-1, keepdims=True) + EPSILON)


def norm_back(grad_normed, inputs, factor, gain):
    weighted = grad_normed * gain
    inner_mean = jnp.mean(weighted * inputs, axis=-1, keepdims=True)
    input_part = factor * weighted - inputs * (factor * factor * factor) * inner_mean
    return (input_part, jnp.sum(grad_normed * inputs * factor, axis=0))


def rounded(values):
    return lax.optimization_barrier(values.astype(jnp.bfloat16)).astype(jnp.float32)


def tile_mask(segment_ids, positions, seg_key, pos_key):
    return (pos_key[None, :] <= positions[:, None]) & (
        (seg_key[None, :] == 0) | (seg_key[None, :] == segment_ids[:, None])
    )


def tile_scores(queries, key_tile, allowed):
    raw_scores = jnp.einsum(
        "nhjd,khd->hjnk", queries, key_tile, preferred_element_type=jnp.float32
    ) * HEAD_DIM ** (-0.5)
    return jnp.where(allowed, raw_scores, -1e30)


def split_tiles(key_all, value_all, seg_all, pos_all):
    tile_count = key_all.shape[0] // KTILE
    key_tiles = key_all.reshape(tile_count, KTILE, KV_HEADS, HEAD_DIM)
    value_tiles = value_all.reshape(tile_count, KTILE, KV_HEADS, HEAD_DIM)
    return (
        key_tiles,
        value_tiles,
        seg_all.reshape(tile_count, KTILE),
        pos_all.reshape(tile_count, KTILE),
    )


def attend_forward(queries, key_all, value_all, seg_all, pos_all, segment_ids, positions):
    local_rows = queries.shape[0]
    head_ratio = HEADS // KV_HEADS
    key_tiles, value_tiles, seg_tiles, pos_tiles = split_tiles(key_all, value_all, seg_all, pos_all)

    def stats_step(state_pair, pieces):
        running_max, running_sum = state_pair
        key_tile, seg_key, pos_key = pieces
        allowed = tile_mask(segment_ids, positions, seg_key, pos_key)
        scores = tile_scores(queries, key_tile, allowed)
        new_max = jnp.maximum(running_max, jnp.max(scores, axis=-1))
        expons = jnp.where(allowed, jnp.exp(scores - new_max[..., None]), 0.0)
        new_sum = running_sum * jnp.exp(running_max - new_max) + jnp.sum(expons, axis=-1)
        return ((new_max, new_sum), None)

    start_max = jnp.full((KV_HEADS, head_ratio, local_rows), -1e30, jnp.float32)
    start_sum = jnp.zeros((KV_HEADS, head_ratio, local_rows), jnp.float32)
    (row_max, row_sum), _ = lax.scan(
        stats_step, (start_max, start_sum), (key_tiles, seg_tiles, pos_tiles)
    )
    log_total = row_max + jnp.log(row_sum)

    def value_step(running, pieces):
        key_tile, value_tile, seg_key, pos_key = pieces
        allowed = tile_mask(segment_ids, positions, seg_key, pos_key)
        scores = tile_scores(queries, key_tile, allowed)
        weights_tile = jnp.where(allowed, jnp.exp(scores - log_total[..., None]), 0.0).astype(
            jnp.bfloat16
        )
        return (
            running
            + jnp.einsum(
                "hjnk,khd->nhjd", weights_tile, value_tile, preferred_element_type=jnp.float32
            ),
            None,
        )

    start_out = jnp.zeros((local_rows, KV_HEADS, head_ratio, HEAD_DIM), jnp.float32)
    output, _ = lax.scan(value_step, start_out, (key_tiles, value_tiles, seg_tiles, pos_tiles))
    return (output, log_total)


def attend_backward(
    queries,
    key_all,
    value_all,
    seg_all,
    pos_all,
    segment_ids,
    positions,
    log_total,
    output_grad,
    output,
):
    key_count = key_all.shape[0]
    key_tiles, value_tiles, seg_tiles, pos_tiles = split_tiles(key_all, value_all, seg_all, pos_all)
    row_delta = jnp.einsum("nhjd,nhjd->hjn", output_grad.astype(jnp.float32), output)

    def grad_step(query_sum, pieces):
        key_tile, value_tile, seg_key, pos_key = pieces
        allowed = tile_mask(segment_ids, positions, seg_key, pos_key)
        scores = tile_scores(queries, key_tile, allowed)
        weights_tile = jnp.where(allowed, jnp.exp(scores - log_total[..., None]), 0.0)
        value_grad = jnp.einsum(
            "hjnk,nhjd->khd",
            weights_tile.astype(jnp.bfloat16),
            output_grad,
            preferred_element_type=jnp.float32,
        )
        weight_grad = jnp.einsum(
            "nhjd,khd->hjnk", output_grad, value_tile, preferred_element_type=jnp.float32
        )
        score_grad = (weights_tile * (weight_grad - row_delta[..., None])).astype(jnp.bfloat16)
        query_sum = query_sum + jnp.einsum(
            "hjnk,khd->nhjd", score_grad, key_tile, preferred_element_type=jnp.float32
        )
        key_grad = jnp.einsum(
            "hjnk,nhjd->khd", score_grad, queries, preferred_element_type=jnp.float32
        )
        return (query_sum, (key_grad, value_grad))

    start_query = jnp.zeros(queries.shape, jnp.float32)
    query_sum, (key_grads, value_grads) = lax.scan(
        grad_step, start_query, (key_tiles, value_tiles, seg_tiles, pos_tiles)
    )
    scale_factor = HEAD_DIM ** (-0.5)
    return (
        query_sum * scale_factor,
        key_grads.reshape(key_count, KW) * scale_factor,
        value_grads.reshape(key_count, KW),
    )


def local(
    tokens,
    segment_ids,
    positions,
    attend_gain,
    query_key_value,
    attend_out,
    feed_gain,
    gate_up,
    down_weight,
    upstream,
):
    local_rows = tokens.shape[0]
    head_ratio = HEADS // KV_HEADS
    inputs = tokens.astype(jnp.float32)
    factor_one = rms_factor(inputs)
    normed_one = (inputs * factor_one * attend_gain).astype(jnp.bfloat16)
    full_qkv, full_out, full_gate_up, full_down = (
        lax.all_gather(query_key_value, "wsh", axis=0, tiled=True),
        lax.all_gather(attend_out, "wsh", axis=0, tiled=True),
        lax.all_gather(gate_up, "wsh", axis=0, tiled=True),
        lax.all_gather(down_weight, "wsh", axis=0, tiled=True),
    )
    projected = jnp.dot(normed_one, full_qkv, preferred_element_type=jnp.float32)
    cosine, sine_table = rope_angles(positions)
    queries = rotate(
        projected[:, :QW].reshape(local_rows, HEADS, HEAD_DIM), cosine, sine_table
    ).astype(jnp.bfloat16)
    queries = queries.reshape(local_rows, KV_HEADS, head_ratio, HEAD_DIM)
    key_local = (
        rotate(
            projected[:, QW : QW + KW].reshape(local_rows, KV_HEADS, HEAD_DIM), cosine, sine_table
        )
        .astype(jnp.bfloat16)
        .reshape(local_rows, KW)
    )
    value_local = projected[:, QW + KW :].astype(jnp.bfloat16)
    key_all, value_all, seg_all, pos_all = (
        lax.all_gather(key_local, ("ctx", "wsh"), axis=0, tiled=True),
        lax.all_gather(value_local, ("ctx", "wsh"), axis=0, tiled=True),
        lax.all_gather(segment_ids, ("ctx", "wsh"), axis=0, tiled=True),
        lax.all_gather(positions, ("ctx", "wsh"), axis=0, tiled=True),
    )
    output, log_total = attend_forward(
        queries, key_all, value_all, seg_all, pos_all, segment_ids, positions
    )
    attended = output.reshape(local_rows, QW).astype(jnp.bfloat16)
    middle = inputs + jnp.dot(attended, full_out, preferred_element_type=jnp.float32)
    factor_two = rms_factor(middle)
    normed_two = (middle * factor_two * feed_gain).astype(jnp.bfloat16)
    gate_value = jnp.dot(normed_two, full_gate_up, preferred_element_type=jnp.float32)
    gate_part = gate_value[:, :FF]
    up_part = gate_value[:, FF:]
    sigmoid_gate = jax.nn.sigmoid(gate_part)
    silu_gate = gate_part * sigmoid_gate
    hidden = (silu_gate * up_part).astype(jnp.bfloat16)
    activations = (middle + jnp.dot(hidden, full_down, preferred_element_type=jnp.float32)).astype(
        jnp.bfloat16
    )
    back_qkv, back_out, back_gate_up, back_down = (
        lax.all_gather(query_key_value, "wsh", axis=0, tiled=True),
        lax.all_gather(attend_out, "wsh", axis=0, tiled=True),
        lax.all_gather(gate_up, "wsh", axis=0, tiled=True),
        lax.all_gather(down_weight, "wsh", axis=0, tiled=True),
    )
    down_grad = jnp.dot(hidden.T, upstream, preferred_element_type=jnp.float32)
    hidden_grad = jnp.dot(upstream, back_down.T, preferred_element_type=jnp.float32)
    gate_grad = hidden_grad * up_part * sigmoid_gate * (1.0 + gate_part * (1.0 - sigmoid_gate))
    up_grad = hidden_grad * silu_gate
    joint_grad = jnp.concatenate([gate_grad, up_grad], axis=1).astype(jnp.bfloat16)
    gate_up_grad = jnp.dot(normed_two.T, joint_grad, preferred_element_type=jnp.float32)
    normed_two_grad = jnp.dot(joint_grad, back_gate_up.T, preferred_element_type=jnp.float32)
    middle_part, feed_gain_grad = norm_back(normed_two_grad, middle, factor_two, feed_gain)
    middle_grad = upstream.astype(jnp.float32) + middle_part
    branch_grad = middle_grad.astype(jnp.bfloat16)
    out_weight_grad = jnp.dot(attended.T, branch_grad, preferred_element_type=jnp.float32)
    attended_grad = jnp.dot(branch_grad, back_out.T, preferred_element_type=jnp.float32).astype(
        jnp.bfloat16
    )
    attended_grad = attended_grad.reshape(local_rows, KV_HEADS, head_ratio, HEAD_DIM)
    query_grad, key_grad_all, value_grad_all = attend_backward(
        queries,
        key_all,
        value_all,
        seg_all,
        pos_all,
        segment_ids,
        positions,
        log_total,
        attended_grad,
        output,
    )
    key_grad, value_grad = (
        lax.psum_scatter(key_grad_all, ("ctx", "wsh"), scatter_dimension=0, tiled=True),
        lax.psum_scatter(value_grad_all, ("ctx", "wsh"), scatter_dimension=0, tiled=True),
    )
    query_back = unrotate(
        rounded(query_grad).reshape(local_rows, HEADS, HEAD_DIM), cosine, sine_table
    ).reshape(local_rows, QW)
    key_back = unrotate(
        rounded(key_grad).reshape(local_rows, KV_HEADS, HEAD_DIM), cosine, sine_table
    ).reshape(local_rows, KW)
    projected_grad = jnp.concatenate(
        [
            query_back.astype(jnp.bfloat16),
            key_back.astype(jnp.bfloat16),
            value_grad.astype(jnp.bfloat16),
        ],
        axis=1,
    )
    qkv_grad = jnp.dot(normed_one.T, projected_grad, preferred_element_type=jnp.float32)
    normed_one_grad = jnp.dot(projected_grad, back_qkv.T, preferred_element_type=jnp.float32)
    input_part, attend_gain_grad = norm_back(normed_one_grad, inputs, factor_one, attend_gain)
    input_grad = middle_grad + input_part
    shares = (
        lax.psum_scatter(qkv_grad, ("ctx", "wsh"), scatter_dimension=0, tiled=True),
        lax.psum_scatter(out_weight_grad, ("ctx", "wsh"), scatter_dimension=0, tiled=True),
        lax.psum_scatter(gate_up_grad, ("ctx", "wsh"), scatter_dimension=0, tiled=True),
        lax.psum_scatter(down_grad, ("ctx", "wsh"), scatter_dimension=0, tiled=True),
        lax.psum_scatter(attend_gain_grad, ("ctx", "wsh"), scatter_dimension=0, tiled=True),
        lax.psum_scatter(feed_gain_grad, ("ctx", "wsh"), scatter_dimension=0, tiled=True),
    )
    shares = (
        lax.psum(shares[0].astype(jnp.bfloat16), "grp").astype(jnp.float32),
        lax.psum(shares[1].astype(jnp.bfloat16), "grp").astype(jnp.float32),
        lax.psum(shares[2].astype(jnp.bfloat16), "grp").astype(jnp.float32),
        lax.psum(shares[3].astype(jnp.bfloat16), "grp").astype(jnp.float32),
        lax.psum(shares[4].astype(jnp.bfloat16), "grp").astype(jnp.float32),
        lax.psum(shares[5].astype(jnp.bfloat16), "grp").astype(jnp.float32),
    )
    return (
        activations,
        input_grad,
        shares[0],
        shares[1],
        shares[2],
        shares[3],
        shares[4],
        shares[5],
    )


def solution(mesh):
    in_specs = (
        P(("grp", "ctx", "wsh"), None),
        P(("grp", "ctx", "wsh")),
        P(("grp", "ctx", "wsh")),
        P(),
        P("wsh", None),
        P("wsh", None),
        P(),
        P("wsh", None),
        P("wsh", None),
        P(("grp", "ctx", "wsh"), None),
    )
    out_specs = (
        P(("grp", "ctx", "wsh"), None),
        P(("grp", "ctx", "wsh"), None),
        P(("ctx", "wsh"), None),
        P(("ctx", "wsh"), None),
        P(("ctx", "wsh"), None),
        P(("ctx", "wsh"), None),
        P(("ctx", "wsh")),
        P(("ctx", "wsh")),
    )
    return jax.shard_map(local, mesh=mesh, in_specs=in_specs, out_specs=out_specs, check_vma=False)
```

profile of v0, /device:TPU:0, one launch (start us, length us, event | category | flops | bytes accessed | tf_op | source)
XLA Modules:
  0.0 1910.9 jit_solution(1182851010017177751)
XLA Ops:
  10.6 56.6 %all-gather.7.cloned.1.call-done = bf16[1152,1920]{1,0:T(8,128)(2,1)} async-done(((bf16[288,1920]{1,0:T(8,128)(2,1)}), bf16[1152,1920]{1,0:T(8,128)(2,1)}) %all-gather.7.cloned.1.call-update) | async-done | bytes 4423696 | tf_op jit(solution)/shard_map/all_gather | solution.py:205
  67.2 3.7 fusion.69
  77.2 76.4 %all-reduce.6 = (s32[3072]{0:T(1024)S(1)}, s32[3072]{0:T(1024)S(1)}) all-reduce(s32[3072]{0:T(1024)S(1)} %dynamic-update-slice, s32[3072]{0:T(1024)S(1)} %dynamic-update-slice.1), channel_id=1, replica_groups=mesh['grp'=2,'ctx'=4,'wsh'=4] {'ctx','wsh'}, use_global_device_ids=true, to_apply=%add | all-reduce | flops 6144 | bytes 49152
  154.3 8.1 reshape.216
  162.4 6.0 copy.46
  168.4 31.3 %all-gather.9.cloned.1.call-done = bf16[3072,384]{1,0:T(8,128)(2,1)} async-done(((bf16[192,384]{1,0:T(8,128)(2,1)}), bf16[3072,384]{1,0:T(8,128)(2,1)}) %all-gather.9.cloned.1.call-update) | async-done | bytes 2359312 | tf_op jit(solution)/shard_map/all_gather | solution.py:226
  199.7 8.1 reshape.215
  207.8 7.2 copy.45
  215.0 24.5 %while.39 = (s32[]{:T(128)}, f32[6,3,192]{2,1,0:T(4,128)S(1)}, f32[6,3,192]{2,1,0:T(4,128)S(1)}, s32[3,1024]{1,0:T(4,128)S(1)}, s32[192]{0:T(256)S(1)}, /*index=...) while((s32[]{:T(128)}, f32[6,3,192]{2,1,0:T(4,128)S(1)}, ...), condition=%wide.region_4.5_spmd.clone, body=%wide.region_1.4_spmd.clone.sunk | while | flops 482101120 | bytes 30485644 | solution.py:111
  218.6 4.6 select_reduce_fusion.2
  226.8 4.5 select_reduce_fusion.2
  235.0 4.6 select_reduce_fusion.2
  240.2 29.6 %while.40 = (s32[]{:T(128)}, f32[192,6,3,64]{0,3,2,1:T(8,128)}, bf16[3,1024,6,64]{1,3,2,0:T(8,128)(2,1)}, s32[3,1024]{1,0:T(4,128)S(1)}, s32[192]{0:T(256)S(1)},...) while((s32[]{:T(128)}, f32[192,6,3,64]{0,3,2,1:T(8,128)}, ...), condition=%wide.region_6.7_spmd.clone, body=%wide.region_5.6_spmd.clone.sunk | while | flops 924894208 | bytes 4674702 | solution.py:132
  242.0 7.8 fusion.126
  251.5 8.5 fusion.126
  261.7 8.2 fusion.126
  272.0 3.7 multiply_reduce_fusion.2
  275.7 101.8 %all-gather.15.cloned.1.call-done = bf16[1152,6144]{1,0:T(8,128)(2,1)} async-done(((bf16[288,6144]{1,0:T(8,128)(2,1)}), bf16[1152,6144]{1,0:T(8,128)(2,1)}) %all-gather.15.cloned.1.call-update) | async-done | bytes 14155792 | tf_op jit(solution)/shard_map/all_gather | solution.py:207
  377.5 11.0 fusion.75
  388.5 67.5 %all-gather.17.cloned.1.call-done = bf16[3072,1152]{1,0:T(8,128)(2,1)} async-done(((bf16[768,1152]{1,0:T(8,128)(2,1)}), bf16[3072,1152]{1,0:T(8,128)(2,1)}) %all-gather.17.cloned.1.call-update) | async-done | bytes 7077904 | tf_op jit(solution)/shard_map/all_gather | solution.py:208
  455.9 8.8 multiply_convert_fusion.1
  464.7 11.3 multiply_reduce_fusion
  483.2 67.5 %while.41 = (s32[]{:T(128)}, f32[192,6,3,64]{0,3,2,1:T(8,128)}, f32[3,1024,6,64]{1,3,2,0:T(8,128)}, f32[3,1024,6,64]{1,3,2,0:T(8,128)}, bf16[3,1024,6,64]{1,3,2,...) while((s32[]{:T(128)}, f32[192,6,3,64]{0,3,2,1:T(8,128)}, ...), condition=%wide.region_10.11_spmd.clone, body=%wide.region_9.10_spmd.clone.sunk | while | flops 2308621312 | bytes 81001752 | solution.py:176
  487.4 6.0 bitcast_dynamic-update-slice_fusion.5
  493.4 7.3 fusion.138
  509.7 6.1 bitcast_dynamic-update-slice_fusion.5
  515.8 7.3 fusion.138
  532.1 6.0 bitcast_dynamic-update-slice_fusion.5
  538.1 7.4 fusion.138
  548.0 2.7 bitcast_dynamic-update-slice_fusion.4
  550.8 5.5 broadcast_multiply_fusion
  556.3 9.2 copy.76
  565.5 10.3 reshape.207
  575.9 9.2 copy.77
  585.1 10.4 reshape.209
  596.9 3.3 fusion.65
  602.1 111.3 %reduce-scatter.19.cloned.1.call-done = f32[192,384]{1,0:T(8,128)} async-done(((f32[3072,384]{1,0:T(8,128)}), f32[192,384]{1,0:T(8,128)}) %reduce-scatter.19.cloned.1.call-update) | async-done | bytes 294928
  714.5 141.3 %reduce-scatter.21.cloned.1.call-done = f32[192,384]{1,0:T(8,128)} async-done(((f32[3072,384]{1,0:T(8,128)}), f32[192,384]{1,0:T(8,128)}) %reduce-scatter.21.cloned.1.call-update) | async-done | bytes 294928
  857.0 5.0 fusion.63
  863.0 8.6 fusion.77
  872.8 12.6 fusion.51
  886.2 115.2 %reduce-scatter.25.cloned.1.call-done = f32[72,1152]{1,0:T(8,128)} async-done(((f32[1152,1152]{1,0:T(8,128)}), f32[72,1152]{1,0:T(8,128)}) %reduce-scatter.25.cloned.1.call-update) | async-done | bytes 331792
  1003.0 170.2 %reduce-scatter.23.cloned.1.call-done = f32[72,1920]{1,0:T(8,128)} async-done(((f32[1152,1920]{1,0:T(8,128)}), f32[72,1920]{1,0:T(8,128)}) %reduce-scatter.23.cloned.1.call-update) | async-done | bytes 552976
  1175.0 224.2 %reduce-scatter.17.cloned.1.call-done = f32[192,1152]{1,0:T(8,128)} async-done(((f32[3072,1152]{1,0:T(8,128)}), f32[192,1152]{1,0:T(8,128)}) %reduce-scatter.17.cloned.1.call-update) | async-done | bytes 884752 | tf_op jit(solution)/shard_map/reduce_scatter | solution.py:305
  1401.1 403.0 %reduce-scatter.15.cloned.1.call-done = f32[72,6144]{1,0:T(8,128)} async-done(((f32[1152,6144]{1,0:T(8,128)}), f32[72,6144]{1,0:T(8,128)}) %reduce-scatter.15.cloned.1.call-update) | async-done | bytes 1769488 | tf_op jit(solution)/shard_map/reduce_scatter | solution.py:304
  1806.6 5.9 fusion.49
  1812.5 4.1 fusion.62
  1816.6 74.8 %all-reduce.7 = (bf16[1152]{0:T(1024)(128)(2,1)S(1)}, bf16[1152]{0:T(1024)(128)(2,1)S(1)}) all-reduce(f32[1152]{0:T(1024)S(1)} %get-tuple-element.388, f32[1152]{0:T(1024)S(1)} %copy-done.29), channel_id=8, replica_groups=mesh['grp'=2,'ctx'=4,'wsh'=4] {'ctx','wsh'}, use_global_device_ids=true, to_apply=%region_23.24.clone | all-reduce | flops 2304 | bytes 13824
  (212 shorter events, 87.9 us)
Async XLA Ops:
  7.2 60.0 %all-gather.7.cloned.1.call-start = ((), (), s32[]{:S(2)}) async-start(), calls=%async_computation.6 | async-start | bytes 5529600 | tf_op jit(solution)/shard_map/all_gather | solution.py:205
  7.9 146.4 %all-gather.11.cloned.1.call-start = ((), (), s32[]{:S(2)}) async-start(), calls=%async_computation.8 | async-start | bytes 2506752 | tf_op jit(solution)/shard_map/all_gather | solution.py:225
  10.4 60.5 %copy-start.26 = (f32[192]{0:T(256)}, f32[192]{0:T(256)S(1)}, u32[]{:S(2)}) copy-start(f32[192]{0:T(256)S(1)} %get-tuple-element.488) | copy-start | bytes 2308
  10.6 143.4 %copy-start.14 = (f32[192,32]{0,1:T(8,128)}, f32[192,32]{0,1:T(8,128)S(1)}, u32[]{:S(2)}) copy-start(f32[192,32]{0,1:T(8,128)S(1)} %get-tuple-element.485) | copy-start | bytes 73732
  10.6 143.4 %copy-start.16 = (f32[192,32]{0,1:T(8,128)}, f32[192,32]{0,1:T(8,128)S(1)}, u32[]{:S(2)}) copy-start(f32[192,32]{0,1:T(8,128)S(1)} %get-tuple-element.486) | copy-start | bytes 73732
  71.2 3.5 copy-start.31
  71.2 4.8 copy-start.19
  72.0 127.7 %all-gather.9.cloned.1.call-start = ((), (), s32[]{:S(2)}) async-start(), calls=%async_computation.7 | async-start | bytes 2506752 | tf_op jit(solution)/shard_map/all_gather | solution.py:226
  72.8 199.3 %all-gather.13.cloned.1.call-start = ((), (), s32[]{:S(2)}) async-start(), calls=%async_computation.9 | async-start | bytes 3317760 | tf_op jit(solution)/shard_map/all_gather | solution.py:206
  73.3 304.2 %all-gather.15.cloned.1.call-start = ((), (), s32[]{:S(2)}) async-start(), calls=%async_computation.10 | async-start | bytes 17694720 | tf_op jit(solution)/shard_map/all_gather | solution.py:207
  73.9 382.0 %all-gather.17.cloned.1.call-start = ((), (), s32[]{:S(2)}) async-start(), calls=%async_computation.11 | async-start | bytes 8847360 | tf_op jit(solution)/shard_map/all_gather | solution.py:208
  74.5 638.9 %reduce-scatter.19.cloned.1.call-start = ((), (), s32[]{:S(2)}) async-start(), calls=%async_computation.14 | async-start | bytes 5013504
  240.2 31.8 %copy-start.7 = (bf16[192,1152]{1,0:T(8,128)(2,1)S(1)}, bf16[192,1152]{1,0:T(8,128)(2,1)}, u32[]{:S(2)}) copy-start(bf16[192,1152]{1,0:T(8,128)(2,1)} %param.16) | copy-start | bytes 1327108
  269.8 118.6 %copy-start.18 = (s32[3,1024]{1,0:T(4,128)}, s32[3,1024]{1,0:T(4,128)S(1)}, u32[]{:S(2)}) copy-start(s32[3,1024]{1,0:T(4,128)S(1)} %get-tuple-element.899) | copy-start | bytes 36868
  269.8 118.6 %copy-start.20 = (s32[192]{0:T(256)}, s32[192]{0:T(256)S(1)}, u32[]{:S(2)}) copy-start(s32[192]{0:T(256)S(1)} %get-tuple-element.902) | copy-start | bytes 2308
  269.8 107.7 %copy-start.21 = (f32[1152]{0:T(1024)S(1)}, f32[1152]{0:T(1024)}, u32[]{:S(2)}) copy-start(f32[1152]{0:T(1024)} %param.22) | copy-start | bytes 13828
  275.7 200.3 %copy-start.24 = (f32[192]{0:T(256)}, f32[192]{0:T(256)S(1)}, u32[]{:S(2)}) copy-start(f32[192]{0:T(256)S(1)} %get-tuple-element.490) | copy-start | bytes 2308
  377.5 78.4 %copy-start.11 = (bf16[192,1152]{1,0:T(8,128)(2,1)S(1)}, bf16[192,1152]{1,0:T(8,128)(2,1)}, u32[]{:S(2)}) copy-start(bf16[192,1152]{1,0:T(8,128)(2,1)} %param.25) | copy-start | bytes 1327108
  455.9 8.8 copy-start.3
  464.7 11.3 copy-start.13
  476.0 2.1 copy-start.9
  487.4 6.1 copy-start.28
  493.4 7.4 copy-start
  503.3 2.7 copy-start.1
  509.7 6.1 copy-start.28
  515.8 7.4 copy-start
  525.7 2.6 copy-start.1
  532.1 6.1 copy-start.28
  538.1 7.4 copy-start
  548.0 2.7 copy-start.1
  575.9 279.9 %reduce-scatter.21.cloned.1.call-start = ((), (), s32[]{:S(2)}) async-start(), calls=%async_computation.15 | async-start | bytes 5013504
  595.5 1.2 copy-start.6
  595.5 1.4 copy-start.10
  595.6 405.8 %reduce-scatter.25.cloned.1.call-start = ((), (), s32[]{:S(2)}) async-start(), calls=%async_computation.17 | async-start | bytes 5640192
  600.2 1.3 copy-start.2
  600.2 1.6 copy-start.15
  600.2 1.6 copy-start.17
  600.2 573.0 %reduce-scatter.23.cloned.1.call-start = ((), (), s32[]{:S(2)}) async-start(), calls=%async_computation.16 | async-start | bytes 9400320
  601.6 255.4 %copy-start.8 = (bf16[192,1152]{1,0:T(8,128)(2,1)S(1)}, bf16[192,1152]{1,0:T(8,128)(2,1)}, u32[]{:S(2)}) copy-start(bf16[192,1152]{1,0:T(8,128)(2,1)} %param.16) | copy-start | bytes 1327108
  601.6 255.4 %copy-start.23 = (f32[1152]{0:T(1024)S(1)}, f32[1152]{0:T(1024)}, u32[]{:S(2)}) copy-start(f32[1152]{0:T(1024)} %param.19) | copy-start | bytes 13828
  601.6 255.4 %copy-start.27 = (f32[192]{0:T(256)S(1)}, f32[192]{0:T(256)}, u32[]{:S(2)}) copy-start(f32[192]{0:T(256)} %copy-done.26) | copy-start | bytes 2308
  862.1 537.1 %reduce-scatter.17.cloned.1.call-start = ((), (), s32[]{:S(2)}) async-start(), calls=%async_computation.13 | async-start | bytes 15040512 | tf_op jit(solution)/shard_map/reduce_scatter | solution.py:305
  871.6 1.2 copy-start.22
  871.6 1.2 copy-start.25
  871.7 932.5 %reduce-scatter.15.cloned.1.call-start = ((), (), s32[]{:S(2)}) async-start(), calls=%async_computation.12 | async-start | bytes 30081024 | tf_op jit(solution)/shard_map/reduce_scatter | solution.py:304
  885.4 1010.8 %all-reduce.12.cloned.1.call-start = ((), (), s32[]{:S(2)}) async-start(), calls=%async_computation.18 | async-start | bytes 3538944 | tf_op jit(solution)/shard_map/psum | solution.py:310
  1812.5 4.1 copy-start.29
  1812.5 82.5 %copy-start.30 = (f32[192]{0:T(256)S(1)}, f32[192]{0:T(256)}, u32[]{:S(2)}) copy-start(f32[192]{0:T(256)} %get-tuple-element.487) | copy-start | bytes 2308
  (3 other events, 3.1 us)
Sparse Core Ops, SparseCore 0:
  9.8 57.3 all-gather.6
  72.1 62.8 all-gather.10
  138.4 61.2 all-gather.8
  201.4 38.7 all-gather.12
  241.9 135.5 all-gather.14
  379.2 76.6 all-gather.16
  576.0 137.3 reduce-scatter.18
  719.4 136.3 reduce-scatter.20
  861.1 140.2 reduce-scatter.24
  1006.9 166.2 reduce-scatter.22
  1179.0 220.1 reduce-scatter.16
  1405.8 398.3 reduce-scatter.14
  1807.4 19.9 all-reduce.11
where the time goes:
time: 1920 us; the launch traced here: 1910 us
  waiting for transfers between devices  1420 us (74%)
  matrix products  173 us (9%)
  blocking collectives  154 us (8%)
  local copies, waits for them, and re-layouts  82.4 us (4%)
  other arithmetic  59.4 us (3%)
    unnamed x17, waiting for transfers between devices  540 us
    reduce_scatter x1, waiting for transfers between devices, local(): lax.psum_scatter(gate_up_grad, ('ctx', 'wsh'), scatter_dimension=0, tiled...  403 us
    reduce_scatter x1, waiting for transfers between devices, local(): lax.psum_scatter(down_grad, ('ctx', 'wsh'), scatter_dimension=0, tiled=True)  224 us
    unnamed x2, blocking collectives  151 us
    all_gather x1, waiting for transfers between devices, local(): lax.all_gather(gate_up, 'wsh', axis=0, tiled=True)  102 us
    all_gather x1, waiting for transfers between devices, local(): lax.all_gather(down_weight, 'wsh', axis=0, tiled=True)  67.5 us
    unnamed x73, local copies, waits for them, and re-layouts  62.7 us
    all_gather x1, waiting for transfers between devices, local(): lax.all_gather(query_key_value, 'wsh', axis=0, tiled=True)  56.6 us
  transfers between devices with their start and end apart: 13, of which 10 were waited for; matrix products, arithmetic and copies ran while one was open for 9% of the time, Pallas kernels for 0%

commit v1 on v0

--- a/solution.py
+++ b/solution.py
@@ -12,6 +12,22 @@
 QW = 1152
 KW = 384
 EPSILON = 1e-05
+
+
+def ring_gather(x, axis, dim):
+    ways, here, step = (lax.axis_size(axis), lax.axis_index(axis), x.shape[dim])
+    dims = [n * ways if d == dim else n for d, n in enumerate(x.shape)]
+    full = lax.dynamic_update_slice_in_dim(jnp.zeros(dims, x.dtype), x, here * step, axis=dim)
+    going_up = going_down = x
+    for far in range(1, ways // 2 + 1):
+        going_up = lax.ppermute(going_up, axis, [(d, (d + 1) % ways) for d in range(ways)])
+        full = lax.dynamic_update_slice_in_dim(full, going_up, (here - far) % ways * step, axis=dim)
+        if 2 * far < ways:
+            going_down = lax.ppermute(going_down, axis, [(d, (d - 1) % ways) for d in range(ways)])
+            full = lax.dynamic_update_slice_in_dim(
+                full, going_down, (here + far) % ways * step, axis=dim
+            )
+    return full
 
 
 def rope_angles(positions):
@@ -205,7 +221,7 @@
         lax.all_gather(query_key_value, "wsh", axis=0, tiled=True),
         lax.all_gather(attend_out, "wsh", axis=0, tiled=True),
         lax.all_gather(gate_up, "wsh", axis=0, tiled=True),
-        lax.all_gather(down_weight, "wsh", axis=0, tiled=True),
+        ring_gather(down_weight, "wsh", 0),
     )
     projected = jnp.dot(normed_one, full_qkv, preferred_element_type=jnp.float32)
     cosine, sine_table = rope_angles(positions)

time: 1920 us -> 2000 us (1.042)
  matrix products: 173 us -> 214 us
  local copies, waits for them, and re-layouts: 82.4 us -> 103 us
  waiting for transfers between devices: 1420 us -> 1440 us
    ppermute x0 -> x3, waiting for transfers between devices: none -> 120 us  [the longest x2 86.3 us: ring_gather(): lax.ppermute(going_up, axis, [(d, (d + 1) % ways) for d in range(ways)])]
    unnamed x17, waiting for transfers between devices: 540 us -> 456 us
  transfers between devices with their start and end apart: 13 -> 16, of which waited for: 10 -> 13; matrix products, arithmetic and copies ran while one was open for 9% -> 10% of each run, Pallas kernels for 0% -> 0%
where the time goes in v1:
time: 2000 us; the launch traced here: 1990 us
  waiting for transfers between devices  1440 us (72%)
  matrix products  214 us (11%)
  blocking collectives  154 us (8%)
  local copies, waits for them, and re-layouts  103 us (5%)
  other arithmetic  59.4 us (3%)
    unnamed x17, waiting for transfers between devices  456 us
    reduce_scatter x1, waiting for transfers between devices, local(): lax.psum_scatter(gate_up_grad, ('ctx', 'wsh'), scatter_dimension=0, tiled...  403 us
    reduce_scatter x1, waiting for transfers between devices, local(): lax.psum_scatter(down_grad, ('ctx', 'wsh'), scatter_dimension=0, tiled=True)  224 us
    unnamed x2, blocking collectives  151 us
    ppermute x2, waiting for transfers between devices, ring_gather(): lax.ppermute(going_up, axis, [(d, (d + 1) % ways) for d in range(ways)])  86.3 us
    all_gather x1, waiting for transfers between devices, local(): lax.all_gather(gate_up, 'wsh', axis=0, tiled=True)  83.2 us
    all_gather x1, waiting for transfers between devices, local(): lax.all_gather(down_weight, 'wsh', axis=0, tiled=True)  67.5 us
    unnamed x73, local copies, waits for them, and re-layouts  61.7 us
  transfers between devices with their start and end apart: 16, of which 13 were waited for; matrix products, arithmetic and copies ran while one was open for 10% of the time, Pallas kernels for 0%

profile of v1, /device:TPU:0, one launch (start us, length us, event | category | flops | bytes accessed | tf_op | source)
XLA Modules:
  0.0 1992.7 jit_solution(2669508710071281563)
XLA Ops:
  10.6 56.6 %all-gather.7.cloned.1.call-done = bf16[1152,1920]{1,0:T(8,128)(2,1)} async-done(((bf16[288,1920]{1,0:T(8,128)(2,1)}), bf16[1152,1920]{1,0:T(8,128)(2,1)}) %all-gather.7.cloned.1.call-update) | async-done | bytes 4423696 | tf_op jit(solution)/shard_map/all_gather | solution.py:221
  76.5 76.5 %all-reduce.6 = (s32[3072]{0:T(1024)S(1)}, s32[3072]{0:T(1024)S(1)}) all-reduce(s32[3072]{0:T(1024)S(1)} %dynamic-update-slice, s32[3072]{0:T(1024)S(1)} %dynamic-update-slice.1), channel_id=1, replica_groups=mesh['grp'=2,'ctx'=4,'wsh'=4] {'ctx','wsh'}, use_global_device_ids=true, to_apply=%add | all-reduce | flops 6144 | bytes 49152
  153.9 8.1 reshape.216
  168.1 31.7 %all-gather.9.cloned.1.call-done = bf16[3072,384]{1,0:T(8,128)(2,1)} async-done(((bf16[192,384]{1,0:T(8,128)(2,1)}), bf16[3072,384]{1,0:T(8,128)(2,1)}) %all-gather.9.cloned.1.call-update) | async-done | bytes 2359312 | tf_op jit(solution)/shard_map/all_gather | solution.py:242
  199.8 8.1 reshape.215
  207.9 7.2 copy.45
  215.1 46.0 %while.39 = (s32[]{:T(128)}, f32[6,3,192]{2,1,0:T(4,128)S(1)}, f32[6,3,192]{2,1,0:T(4,128)S(1)}, s32[3,1024]{1,0:T(4,128)S(1)}, s32[192]{0:T(256)S(1)}, /*index=...) while((s32[]{:T(128)}, f32[6,3,192]{2,1,0:T(4,128)S(1)}, ...), condition=%wide.region_4.5_spmd.clone, body=%wide.region_1.4_spmd.clone.sunk | while | flops 482101120 | bytes 30485636 | solution.py:127
  215.4 6.4 fusion.121
  221.8 8.0 select_reduce_fusion.2
  230.3 6.4 fusion.121
  236.7 7.6 select_reduce_fusion.2
  244.7 8.0 fusion.121
  252.7 8.4 select_reduce_fusion.2
  261.2 27.3 %while.40 = (s32[]{:T(128)}, f32[192,6,3,64]{0,3,2,1:T(8,128)}, bf16[3,1024,6,64]{1,3,2,0:T(8,128)(2,1)}, s32[3,1024]{1,0:T(4,128)S(1)}, s32[192]{0:T(256)S(1)},...) while((s32[]{:T(128)}, f32[192,6,3,64]{0,3,2,1:T(8,128)}, ...), condition=%wide.region_6.7_spmd.clone, body=%wide.region_5.6_spmd.clone.sunk | while | flops 924894208 | bytes 4674183 | solution.py:148
  262.2 7.7 fusion.126
  271.0 8.2 fusion.126
  280.1 8.2 fusion.126
  294.4 83.2 %all-gather.15.cloned.1.call-done = bf16[1152,6144]{1,0:T(8,128)(2,1)} async-done(((bf16[288,6144]{1,0:T(8,128)(2,1)}), bf16[1152,6144]{1,0:T(8,128)(2,1)}) %all-gather.15.cloned.1.call-update) | async-done | bytes 14155792 | tf_op jit(solution)/shard_map/all_gather | solution.py:223
  377.6 11.0 fusion.75
  388.5 67.5 %all-gather.17.cloned.1.call-done = bf16[3072,1152]{1,0:T(8,128)(2,1)} async-done(((bf16[768,1152]{1,0:T(8,128)(2,1)}), bf16[3072,1152]{1,0:T(8,128)(2,1)}) %all-gather.17.cloned.1.call-update) | async-done | bytes 7077904 | tf_op jit(solution)/shard_map/all_gather | solution.py:266
  456.0 8.8 multiply_convert_fusion.1
  464.8 11.3 multiply_reduce_fusion
  482.9 98.4 %while.41 = (s32[]{:T(128)}, f32[192,6,3,64]{0,3,2,1:T(8,128)}, f32[3,1024,6,64]{1,3,2,0:T(8,128)}, f32[3,1024,6,64]{1,3,2,0:T(8,128)}, bf16[3,1024,6,64]{1,3,2,...) while((s32[]{:T(128)}, f32[192,6,3,64]{0,3,2,1:T(8,128)}, ...), condition=%wide.region_10.11_spmd.clone, body=%wide.region_9.10_spmd.clone.sunk | while | flops 2308621312 | bytes 158783216 | solution.py:192
  485.7 8.0 fusion.138
  499.2 6.4 fusion.139
  505.6 10.2 bitcast_dynamic-update-slice_fusion.5
  518.2 8.0 fusion.138
  531.7 6.7 fusion.139
  538.4 10.2 bitcast_dynamic-update-slice_fusion.5
  550.9 8.0 fusion.138
  564.5 6.7 fusion.139
  571.2 10.1 bitcast_dynamic-update-slice_fusion.5
  586.7 9.2 copy.76
  595.9 10.4 reshape.207
  606.4 9.4 copy.77
  615.7 10.4 reshape.209
  632.7 111.2 %reduce-scatter.19.cloned.1.call-done = f32[192,384]{1,0:T(8,128)} async-done(((f32[3072,384]{1,0:T(8,128)}), f32[192,384]{1,0:T(8,128)}) %reduce-scatter.19.cloned.1.call-update) | async-done | bytes 294928
  745.1 141.3 %reduce-scatter.21.cloned.1.call-done = f32[192,384]{1,0:T(8,128)} async-done(((f32[3072,384]{1,0:T(8,128)}), f32[192,384]{1,0:T(8,128)}) %reduce-scatter.21.cloned.1.call-update) | async-done | bytes 294928
  893.7 8.5 fusion.77
  903.4 12.6 fusion.51
  919.1 49.5 %collective-permute-done = bf16[768,1152]{1,0:T(8,128)(2,1)} collective-permute-done((bf16[768,1152]{1,0:T(8,128)(2,1)}, bf16[768,1152]{1,0:T(8,128)(2,1)}, u32[]{:S(2)}, u32[]{:S(2)}) %collective-permute-start) | collective-permute-done | bytes 1769504 | tf_op jit(solution)/shard_map/ppermute | solution.py:23
  976.9 34.0 %collective-permute-done.1 = bf16[768,1152]{1,0:T(8,128)(2,1)} collective-permute-done((bf16[768,1152]{1,0:T(8,128)(2,1)}, bf16[768,1152]{1,0:T(8,128)(2,1)}, u32[]{:S(2)}, u32[]{:S(2)}) %collective-permute-start.1) | collective-permute-done | bytes 1769504 | tf_op jit(solution)/shard_map/ppermute | solution.py:26
  1013.9 36.8 %collective-permute-done.2 = bf16[768,1152]{1,0:T(8,128)(2,1)} collective-permute-done((bf16[768,1152]{1,0:T(8,128)(2,1)}, bf16[768,1152]{1,0:T(8,128)(2,1)}, u32[]{:S(2)}, u32[]{:S(2)}) %collective-permute-start.2) | collective-permute-done | bytes 1769504 | tf_op jit(solution)/shard_map/ppermute | solution.py:23
  1053.5 31.0 %reduce-scatter.25.cloned.1.call-done = f32[72,1152]{1,0:T(8,128)} async-done(((f32[1152,1152]{1,0:T(8,128)}), f32[72,1152]{1,0:T(8,128)}) %reduce-scatter.25.cloned.1.call-update) | async-done | bytes 331792
  1086.2 170.0 %reduce-scatter.23.cloned.1.call-done = f32[72,1920]{1,0:T(8,128)} async-done(((f32[1152,1920]{1,0:T(8,128)}), f32[72,1920]{1,0:T(8,128)}) %reduce-scatter.23.cloned.1.call-update) | async-done | bytes 552976
  1258.0 224.2 %reduce-scatter.17.cloned.1.call-done = f32[192,1152]{1,0:T(8,128)} async-done(((f32[3072,1152]{1,0:T(8,128)}), f32[192,1152]{1,0:T(8,128)}) %reduce-scatter.17.cloned.1.call-update) | async-done | bytes 884752 | tf_op jit(solution)/shard_map/reduce_scatter | solution.py:321
  1484.2 402.6 %reduce-scatter.15.cloned.1.call-done = f32[72,6144]{1,0:T(8,128)} async-done(((f32[1152,6144]{1,0:T(8,128)}), f32[72,6144]{1,0:T(8,128)}) %reduce-scatter.15.cloned.1.call-update) | async-done | bytes 1769488 | tf_op jit(solution)/shard_map/reduce_scatter | solution.py:320
  1899.3 74.8 %all-reduce.7 = (bf16[1152]{0:T(1024)(128)(2,1)S(1)}, bf16[1152]{0:T(1024)(128)(2,1)S(1)}) all-reduce(f32[1152]{0:T(1024)S(1)} %get-tuple-element.388, f32[1152]{0:T(1024)S(1)} %copy-done.28), channel_id=8, replica_groups=mesh['grp'=2,'ctx'=4,'wsh'=4] {'ctx','wsh'}, use_global_device_ids=true, to_apply=%region_23.24.clone | all-reduce | flops 2304 | bytes 13824
  (217 shorter events, 126.7 us)
Async XLA Ops:
  7.2 60.0 %all-gather.7.cloned.1.call-start = ((), (), s32[]{:S(2)}) async-start(), calls=%async_computation.6 | async-start | bytes 5529600 | tf_op jit(solution)/shard_map/all_gather | solution.py:221
  7.9 145.9 %all-gather.11.cloned.1.call-start = ((), (), s32[]{:S(2)}) async-start(), calls=%async_computation.8 | async-start | bytes 2506752 | tf_op jit(solution)/shard_map/all_gather | solution.py:241
  10.4 60.5 %copy-start.26 = (f32[192]{0:T(256)}, f32[192]{0:T(256)S(1)}, u32[]{:S(2)}) copy-start(f32[192]{0:T(256)S(1)} %get-tuple-element.488) | copy-start | bytes 2308
  10.6 142.9 %copy-start.14 = (f32[192,32]{0,1:T(8,128)}, f32[192,32]{0,1:T(8,128)S(1)}, u32[]{:S(2)}) copy-start(f32[192,32]{0,1:T(8,128)S(1)} %get-tuple-element.485) | copy-start | bytes 73732
  10.6 142.9 %copy-start.16 = (f32[192,32]{0,1:T(8,128)}, f32[192,32]{0,1:T(8,128)S(1)}, u32[]{:S(2)}) copy-start(f32[192,32]{0,1:T(8,128)S(1)} %get-tuple-element.486) | copy-start | bytes 73732
  70.9 3.7 copy-start.30
  70.9 5.1 copy-start.18
  70.9 5.3 copy-start.21
  72.0 127.8 %all-gather.9.cloned.1.call-start = ((), (), s32[]{:S(2)}) async-start(), calls=%async_computation.7 | async-start | bytes 2506752 | tf_op jit(solution)/shard_map/all_gather | solution.py:242
  72.8 217.9 %all-gather.13.cloned.1.call-start = ((), (), s32[]{:S(2)}) async-start(), calls=%async_computation.9 | async-start | bytes 3317760 | tf_op jit(solution)/shard_map/all_gather | solution.py:222
  73.4 304.2 %all-gather.15.cloned.1.call-start = ((), (), s32[]{:S(2)}) async-start(), calls=%async_computation.10 | async-start | bytes 17694720 | tf_op jit(solution)/shard_map/all_gather | solution.py:223
  73.9 382.1 %all-gather.17.cloned.1.call-start = ((), (), s32[]{:S(2)}) async-start(), calls=%async_computation.11 | async-start | bytes 8847360 | tf_op jit(solution)/shard_map/all_gather | solution.py:266
  74.5 669.4 %reduce-scatter.19.cloned.1.call-start = ((), (), s32[]{:S(2)}) async-start(), calls=%async_computation.14 | async-start | bytes 5013504
  261.2 29.5 %copy-start.7 = (bf16[192,1152]{1,0:T(8,128)(2,1)S(1)}, bf16[192,1152]{1,0:T(8,128)(2,1)}, u32[]{:S(2)}) copy-start(bf16[192,1152]{1,0:T(8,128)(2,1)} %param.16) | copy-start | bytes 1327108
  288.5 89.1 %copy-start.19 = (f32[1152]{0:T(1024)S(1)}, f32[1152]{0:T(1024)}, u32[]{:S(2)}) copy-start(f32[1152]{0:T(1024)} %param.22) | copy-start | bytes 13828
  294.4 181.7 %copy-start.24 = (f32[192]{0:T(256)}, f32[192]{0:T(256)S(1)}, u32[]{:S(2)}) copy-start(f32[192]{0:T(256)S(1)} %get-tuple-element.490) | copy-start | bytes 2308
  377.6 78.4 %copy-start.11 = (bf16[192,1152]{1,0:T(8,128)(2,1)S(1)}, bf16[192,1152]{1,0:T(8,128)(2,1)}, u32[]{:S(2)}) copy-start(bf16[192,1152]{1,0:T(8,128)(2,1)} %param.25) | copy-start | bytes 1327108
  456.0 8.8 copy-start.3
  464.8 11.3 copy-start.13
  485.7 8.1 copy-start
  493.7 2.8 copy-start.1
  518.2 8.1 copy-start
  526.2 2.8 copy-start.1
  550.9 8.1 copy-start
  559.0 2.8 copy-start.1
  606.3 280.1 %reduce-scatter.21.cloned.1.call-start = ((), (), s32[]{:S(2)}) async-start(), calls=%async_computation.15 | async-start | bytes 5013504
  626.1 1.2 copy-start.6
  626.1 1.3 copy-start.9
  626.2 458.4 %reduce-scatter.25.cloned.1.call-start = ((), (), s32[]{:S(2)}) async-start(), calls=%async_computation.17 | async-start | bytes 5640192
  630.8 1.3 copy-start.2
  630.8 1.6 copy-start.15
  630.8 1.6 copy-start.17
  630.9 625.3 %reduce-scatter.23.cloned.1.call-start = ((), (), s32[]{:S(2)}) async-start(), calls=%async_computation.16 | async-start | bytes 9400320
  632.1 255.5 %copy-start.8 = (bf16[192,1152]{1,0:T(8,128)(2,1)S(1)}, bf16[192,1152]{1,0:T(8,128)(2,1)}, u32[]{:S(2)}) copy-start(bf16[192,1152]{1,0:T(8,128)(2,1)} %param.16) | copy-start | bytes 1327108
  632.1 255.5 %copy-start.22 = (f32[1152]{0:T(1024)S(1)}, f32[1152]{0:T(1024)}, u32[]{:S(2)}) copy-start(f32[1152]{0:T(1024)} %param.19) | copy-start | bytes 13828
  632.1 255.5 %copy-start.27 = (f32[192]{0:T(256)S(1)}, f32[192]{0:T(256)}, u32[]{:S(2)}) copy-start(f32[192]{0:T(256)} %copy-done.26) | copy-start | bytes 2308
  892.7 589.5 %reduce-scatter.17.cloned.1.call-start = ((), (), s32[]{:S(2)}) async-start(), calls=%async_computation.13 | async-start | bytes 15040512 | tf_op jit(solution)/shard_map/reduce_scatter | solution.py:321
  902.2 1.2 copy-start.20
  902.2 1.2 copy-start.25
  902.2 984.6 %reduce-scatter.15.cloned.1.call-start = ((), (), s32[]{:S(2)}) async-start(), calls=%async_computation.12 | async-start | bytes 30081024 | tf_op jit(solution)/shard_map/reduce_scatter | solution.py:320
  916.0 1062.9 %all-reduce.12.cloned.1.call-start = ((), (), s32[]{:S(2)}) async-start(), calls=%async_computation.18 | async-start | bytes 3538944 | tf_op jit(solution)/shard_map/psum | solution.py:326
  916.1 52.4 %collective-permute-start = (bf16[768,1152]{1,0:T(8,128)(2,1)}, bf16[768,1152]{1,0:T(8,128)(2,1)}, u32[]{:S(2)}, u32[]{:S(2)}) collective-permute-start(bf16[768,1152]{1,0:T(8,128)(2,1)} %param.24), channel_id=1, source_target_pairs={{0,1},{1,2},{2,3},{3,0},{4,5},{5,6},{6,7},{7,4},{8,9},{9,10},{10,1... | collective-permute-start | bytes 5308424 | tf_op jit(solution)/shard_map/ppermute | solution.py:23
  917.7 93.3 %collective-permute-start.1 = (bf16[768,1152]{1,0:T(8,128)(2,1)}, bf16[768,1152]{1,0:T(8,128)(2,1)}, u32[]{:S(2)}, u32[]{:S(2)}) collective-permute-start(bf16[768,1152]{1,0:T(8,128)(2,1)} %param.24), channel_id=1, source_target_pairs={{0,3},{1,0},{2,1},{3,2},{4,7},{5,4},{6,5},{7,6},{8,11},{9,8},{10,9... | collective-permute-start | bytes 5308424 | tf_op jit(solution)/shard_map/ppermute | solution.py:26
  968.5 82.2 %collective-permute-start.2 = (bf16[768,1152]{1,0:T(8,128)(2,1)}, bf16[768,1152]{1,0:T(8,128)(2,1)}, u32[]{:S(2)}, u32[]{:S(2)}) collective-permute-start(bf16[768,1152]{1,0:T(8,128)(2,1)} %collective-permute-done), channel_id=1, source_target_pairs={{0,1},{1,2},{2,3},{3,0},{4,5},{5,6},{6,7},{7,4},{8,9},{9,10},{10,1... | collective-permute-start | bytes 5308424 | tf_op jit(solution)/shard_map/ppermute | solution.py:23
  969.4 3.4 copy-start.10
  1895.2 4.1 copy-start.28
  1895.2 82.5 %copy-start.29 = (f32[192]{0:T(256)S(1)}, f32[192]{0:T(256)}, u32[]{:S(2)}) copy-start(f32[192]{0:T(256)} %get-tuple-element.487) | copy-start | bytes 2308
  1978.9 6.3 copy-start.23
  (3 other events, 3.1 us)
Sparse Core Ops, SparseCore 0:
  9.8 57.3 all-gather.6
  72.1 62.7 all-gather.10
  138.3 61.4 all-gather.8
  201.5 38.7 all-gather.12
  241.9 135.6 all-gather.14
  379.3 76.6 all-gather.16
  606.4 137.4 reduce-scatter.18
  750.0 136.3 reduce-scatter.20
  891.6 192.8 reduce-scatter.24
  1090.1 166.0 reduce-scatter.22
  1262.0 220.1 reduce-scatter.16
  1488.8 397.9 reduce-scatter.14
  1890.1 19.9 all-reduce.11
